TPU v7x, 256 devices: a whole 4x4x8 slice. The times are simulated.
256 devices in a mesh: col: 64 (over y, z, core), row: 4 (over x).
Axes of the slice: x: 4, y: 4, z: 8, core: 2. Of those that a mesh axis runs over, the one named last changes fastest.
Arguments:
- r_slab: float32 [1024, 16384], P('row', 'col'), may hold values from -4 to 8, as said below
- arc_rows: float32 [4096, 16384], P('row', 'col'), may hold values from -6 to 6
- arc_blocks: int32 [32, 64], P('row', 'col'), may hold values 0 or 1
Outputs:
- r_updated: float32 [1024, 16384], P('row', 'col')
Inputs may be any that keep to these rules, and one draw needn't show every extreme that they name: r_slab is zero wherever an entry's global column index is below its row index, and its diagonal is positive.
All inputs are finite; a program needn't handle non-finite values. No bound on the sum of `arc_blocks` on one device may be relied on, other than what follows from the above.
Results may differ from a plain program's by a relative error of at most 0.000098.
Values sent between devices are 32-bit elements; how exact they have to be, the bound alone decides.
A program may use at most 64 MiB of HBM per device.

v0:
```python
import jax
import jax.numpy as jnp
from jax import lax
from jax.sharding import PartitionSpec as P

B = 256
P_SIZE = 4
ARC_ROWS = 128
HI = lax.Precision.HIGHEST


def inner_dot(left, right):
    return lax.dot_general(left, right, (((0,), (0,)), ((), ())), precision=HI)


def plain_dot(left, right):
    return jnp.dot(left, right, precision=HI)


def on_device(r_slab, arc_rows, arc_blocks):
    n_col = lax.axis_size("col")
    col_index = lax.axis_index("col")
    row_index = lax.axis_index("row")
    n_arcs, blocks_here = arc_blocks.shape
    lead = P_SIZE * B
    live = arc_blocks.astype(jnp.float32)
    masked = (arc_rows.reshape(n_arcs, ARC_ROWS, blocks_here, B) * live[:, None, :, None]).reshape(
        arc_rows.shape
    )
    stacked = jnp.concatenate([r_slab, masked], axis=0)
    height = stacked.shape[0]
    part = height // n_col
    pieces = stacked.reshape(n_col, part, B)
    pieces = lax.all_to_all(pieces, "col", split_axis=0, concat_axis=0, tiled=True)
    mine = pieces[:P_SIZE]
    panels = lax.all_gather(mine, "col")
    panels = panels.transpose(0, 2, 1, 3).reshape(height, lead)
    share = lead // n_col
    own = lax.dynamic_slice(panels, (0, col_index * share), (height, share))
    gram_part = lax.psum(inner_dot(own, panels), "row")
    gram = lax.all_gather(gram_part, "col", tiled=True)
    rhs = lax.psum(inner_dot(panels, stacked), "row")
    lower = jnp.linalg.cholesky(gram, symmetrize_input=False)
    factor = jax.scipy.linalg.solve_triangular(lower, rhs, lower=True)
    mine_out = lax.dynamic_slice(factor, (row_index * B, 0), (B, B))
    row_ids = row_index * B + lax.broadcasted_iota(jnp.int32, (B, B), 0)
    col_ids = col_index * B + lax.broadcasted_iota(jnp.int32, (B, B), 1)
    return jnp.where(col_ids >= row_ids, mine_out, jnp.zeros_like(mine_out))


def solution(mesh):
    return jax.shard_map(
        on_device,
        mesh=mesh,
        in_specs=(P("row", "col"), P("row", "col"), P("row", "col")),
        out_specs=P("row", "col"),
        check_vma=False,
    )
```

profile of v0, /device:TPU:1, one launch (start us, length us, event | category | flops | bytes accessed | tf_op | source)
XLA Modules:
  0.0 636.5 jit_solution(12063077370027670616)
XLA Ops:
  7.3 1.4 broadcast_multiply_fusion
  8.7 2.1 pad_maximum_fusion
  10.8 1.4 reshape.90
  12.2 52.7 %all_to_all.5 = f32[64,20,256]{2,1,0:T(8,128)S(1)} all-to-all(f32[64,20,256]{2,1,0:T(8,128)S(1)} %reshape.90), channel_id=1, replica_groups=mesh['col'=64,'row'=4] {'col'}, dimensions={0} | all-to-all | bytes 2621440 | tf_op jit(solution)/shard_map/all_to_all | solution.py:34
  65.7 78.4 %all-gather.6.cloned.1.call-done = f32[256,20,256]{2,1,0:T(8,128)} async-done(((f32[4,20,256]{2,1,0:T(8,128)}), f32[256,20,256]{2,1,0:T(8,128)}) %all-gather.6.cloned.1.call-update) | async-done | bytes 5242896 | tf_op jit(solution)/shard_map/all_gather | solution.py:36
  144.1 5.2 copy.5
  150.5 9.5 %fusion.63 = f32[1024,256]{1,0:T(8,128)} fusion(f32[1280,1024]{1,0:T(8,128)S(1)} %bitcast.108, f32[1024,256]{1,0:T(8,128)S(1)} %broadcast_multiply_fusion, f32[256,256]{1,0:T(8,128)S(1)} %copy-done), kind=kOutput, calls=%fused_computation.162 | convolution fusion | flops 4026859520 | bytes 7602176 | tf_op jit(solution)/shard_map/dot_general | solution.py:13
  160.1 14.3 %fusion.5 = f32[16,1024]{1,0:T(8,128)} fusion(f32[1280,1024]{1,0:T(8,128)S(1)} %bitcast.109, s32[]{:T(128)S(6)} %select_n.14), kind=kOutput, calls=%fused_computation.31 | convolution fusion | flops 251658240 | bytes 5963780 | tf_op jit(solution)/shard_map/dot_general | solution.py:13
  174.4 46.4 %all-reduce.4.cloned.1.call-done = (f32[1024,256]{1,0:T(8,128)}, f32[16,1024]{1,0:T(8,128)}) async-done(((f32[1024,256]{1,0:T(8,128)}, f32[16,1024]{1,0:T(8,128)}), (f32[1024,256]{1,0:T(8,128)}, f32[16,1024]{1,0:T(8,128)})) %all-reduce.4.cloned.1.call-update) | async-done | bytes 1114128 | tf_op jit(solution)/shard_map/psum | solution.py:42
  220.8 84.7 %all-gather.4.cloned.1.call-done = f32[1024,1024]{1,0:T(8,128)} async-done(((f32[16,1024]{1,0:T(8,128)}), f32[1024,1024]{1,0:T(8,128)}) %all-gather.4.cloned.1.call-update) | async-done | bytes 4194320 | tf_op jit(solution)/shard_map/all_gather | solution.py:41
  306.4 11.7 %cholesky.223 = f32[128,128]{1,0:T(8,128)S(1)} custom-call(f32[128,128]{1,0:T(8,128)S(1)} %cholesky.580), custom_call_target="Cholesky" | custom-call | tf_op jit(solution)/shard_map/jit(cholesky)/cholesky | solution.py:43
  318.1 9.8 %custom-call.63 = f32[1,128,128]{1,2,0:T(8,128)S(1)} custom-call(f32[1,128,128]{2,1,0:T(8,128)S(1)} %get-tuple-element.71), custom_call_target="InvertDiagBlocksLowerTriangular" | custom-call | tf_op jit(solution)/shard_map/jit(cholesky)/cholesky | solution.py:43
  328.0 2.5 cholesky.255
  330.5 2.4 constant_dynamic-update-slice_fusion.31
  332.8 1.5 convolution_subtract_fusion
  334.4 11.7 %cholesky.244 = f32[128,128]{1,0:T(8,128)S(1)} custom-call(f32[128,128]{1,0:T(8,128)S(1)} %cholesky.584), custom_call_target="Cholesky" | custom-call | tf_op jit(solution)/shard_map/jit(cholesky)/cholesky | solution.py:43
  346.8 10.2 %custom-call.64 = f32[1,128,128]{1,2,0:T(8,128)S(1)} custom-call(f32[1,128,128]{2,1,0:T(8,128)S(1)} %get-tuple-element.68), custom_call_target="InvertDiagBlocksLowerTriangular" | custom-call | tf_op jit(solution)/shard_map/jit(cholesky)/cholesky | solution.py:43
  358.2 2.1 convolution_subtract_fusion.1
  360.3 11.7 %cholesky.468 = f32[128,128]{1,0:T(8,128)S(1)} custom-call(f32[128,128]{1,0:T(8,128)S(1)} %cholesky.589), custom_call_target="Cholesky" | custom-call | tf_op jit(solution)/shard_map/jit(cholesky)/cholesky | solution.py:43
  373.4 9.8 %custom-call.65 = f32[1,128,128]{1,2,0:T(8,128)S(1)} custom-call(f32[1,128,128]{2,1,0:T(8,128)S(1)} %get-tuple-element.65), custom_call_target="InvertDiagBlocksLowerTriangular" | custom-call | tf_op jit(solution)/shard_map/jit(cholesky)/cholesky | solution.py:43
  384.3 2.3 convolution_subtract_fusion.2
  386.7 11.9 %cholesky.487 = f32[128,128]{1,0:T(8,128)S(1)} custom-call(f32[128,128]{1,0:T(8,128)S(1)} %cholesky.594), custom_call_target="Cholesky" | custom-call | tf_op jit(solution)/shard_map/jit(cholesky)/cholesky | solution.py:43
  399.9 9.8 %custom-call.66 = f32[1,128,128]{1,2,0:T(8,128)S(1)} custom-call(f32[1,128,128]{2,1,0:T(8,128)S(1)} %get-tuple-element.62), custom_call_target="InvertDiagBlocksLowerTriangular" | custom-call | tf_op jit(solution)/shard_map/jit(cholesky)/cholesky | solution.py:43
  410.8 2.3 convolution_subtract_fusion.3
  413.2 11.7 %cholesky.506 = f32[128,128]{1,0:T(8,128)S(1)} custom-call(f32[128,128]{1,0:T(8,128)S(1)} %cholesky.599), custom_call_target="Cholesky" | custom-call | tf_op jit(solution)/shard_map/jit(cholesky)/cholesky | solution.py:43
  426.2 9.8 %custom-call.67 = f32[1,128,128]{1,2,0:T(8,128)S(1)} custom-call(f32[1,128,128]{2,1,0:T(8,128)S(1)} %get-tuple-element.59), custom_call_target="InvertDiagBlocksLowerTriangular" | custom-call | tf_op jit(solution)/shard_map/jit(cholesky)/cholesky | solution.py:43
  437.1 2.5 convolution_subtract_fusion.4
  439.6 11.7 %cholesky.526 = f32[128,128]{1,0:T(8,128)S(1)} custom-call(f32[128,128]{1,0:T(8,128)S(1)} %cholesky.604), custom_call_target="Cholesky" | custom-call | tf_op jit(solution)/shard_map/jit(cholesky)/cholesky | solution.py:43
  452.7 9.8 %custom-call.68 = f32[1,128,128]{1,2,0:T(8,128)S(1)} custom-call(f32[1,128,128]{2,1,0:T(8,128)S(1)} %get-tuple-element.56), custom_call_target="InvertDiagBlocksLowerTriangular" | custom-call | tf_op jit(solution)/shard_map/jit(cholesky)/cholesky | solution.py:43
  463.4 2.0 convolution_subtract_fusion.11
  465.5 11.7 %cholesky.546 = f32[128,128]{1,0:T(8,128)S(1)} custom-call(f32[128,128]{1,0:T(8,128)S(1)} %cholesky.609), custom_call_target="Cholesky" | custom-call | tf_op jit(solution)/shard_map/jit(cholesky)/cholesky | solution.py:43
  478.5 10.2 %custom-call.69 = f32[1,128,128]{1,2,0:T(8,128)S(1)} custom-call(f32[1,128,128]{2,1,0:T(8,128)S(1)} %get-tuple-element.53), custom_call_target="InvertDiagBlocksLowerTriangular" | custom-call | tf_op jit(solution)/shard_map/jit(cholesky)/cholesky | solution.py:43
  489.5 1.8 convolution_subtract_fusion.13
  491.3 11.7 %cholesky.564 = f32[128,128]{1,0:T(8,128)S(1)} custom-call(f32[128,128]{1,0:T(8,128)S(1)} %convolution_subtract_fusion.13), custom_call_target="Cholesky" | custom-call | tf_op jit(solution)/shard_map/jit(cholesky)/cholesky | solution.py:43
  510.1 4.9 select_select_fusion
  515.0 23.1 %while.1 = (s32[]{:T(128)}, f32[1024,1024]{1,0:T(8,128)}, s32[8,2]{0,1:T(2,128)S(1)}, f32[8,128,128]{2,1,0:T(8,128)S(1)}, s32[]{:T(128)}) while((s32[]{:T(128)}, f32[1024,1024]{1,0:T(8,128)}, s32[8,2]{0,1:T(2,128)S(1)}, f32[8,128,128]{2,1,0:T(8,128)S(1)}, s32[]{:T(128)}) %tuple.58), condition=%wide.while_cond, body=%wide.while_body.sunk | while | flops 2 | bytes 131181 | solution.py:44
  515.7 2.3 bitcast_dynamic-update-slice_fusion.2
  518.6 2.3 bitcast_dynamic-update-slice_fusion.2
  521.5 2.3 bitcast_dynamic-update-slice_fusion.2
  524.4 2.3 bitcast_dynamic-update-slice_fusion.2
  527.3 2.3 bitcast_dynamic-update-slice_fusion.2
  530.2 2.3 bitcast_dynamic-update-slice_fusion.2
  533.0 2.3 bitcast_dynamic-update-slice_fusion.2
  535.9 2.2 bitcast_dynamic-update-slice_fusion.2
  538.1 78.6 %custom-call.70 = f32[8,128,128]{1,2,0:T(8,128)S(1)} custom-call(f32[8,128,128]{2,1,0:T(8,128)S(1)} %get-tuple-element.12), custom_call_target="InvertDiagBlocksLowerTriangular" | custom-call | tf_op jit(solution)/shard_map/jit(_solve_triangular)/triangular_solve | solution.py:44
  623.4 1.5 convolution_subtract_fusion.5
  625.2 1.5 convolution_subtract_fusion.9
  627.0 1.6 convolution_subtract_fusion.12
  (75 shorter events, 32.4 us)
Async XLA Ops:
  6.5 137.5 %all-gather.6.cloned.1.call-start = ((), (), s32[]{:S(2)}) async-start(), calls=%async_computation.2 | async-start | bytes 6389760 | tf_op jit(solution)/shard_map/all_gather | solution.py:36
  65.6 155.2 %all-reduce.4.cloned.1.call-start = ((), (), s32[]{:S(2)}) async-start(), calls=%async_computation.3 | async-start | bytes 2228224 | tf_op jit(solution)/shard_map/psum | solution.py:42
  149.2 1.3 copy-start
  174.4 131.2 %all-gather.4.cloned.1.call-start = ((), (), s32[]{:S(2)}) async-start(), calls=%async_computation.1 | async-start | bytes 4259840 | tf_op jit(solution)/shard_map/all_gather | solution.py:41
  510.1 106.6 %copy-start.1 = (f32[1024,256]{1,0:T(8,128)S(1)}, f32[1024,256]{1,0:T(8,128)}, u32[]{:S(2)}) copy-start(f32[1024,256]{1,0:T(8,128)} %get-tuple-element.21) | copy-start | bytes 3145732
Sparse Core Ops, SparseCore 0:
  65.7 78.2 all-gather.5
  174.5 46.2 all-reduce.3
  223.9 81.5 all-gather.3
where the time goes:
time: 647 us; the launch traced here: 636 us
  other arithmetic  261 us (40%)
  waiting for transfers between devices  210 us (32%)
  matrix products  59.2 us (9%)
  blocking collectives  52.7 us (8%)
  local copies, waits for them, and re-layouts  34.8 us (5%)
  between operations  18.8 us (3%)
    another operation x30, other arithmetic, on_device(): lower = jnp.linalg.cholesky(gram, symmetrize_input=False)  173 us
    all_gather x1, waiting for transfers between devices, on_device(): gram = lax.all_gather(gram_part, 'col', tiled=True)  84.7 us
    another operation x3, other arithmetic, on_device(): factor = jax.scipy.linalg.solve_triangular(lower, rhs, lower=True)  83.5 us
    all_gather x1, waiting for transfers between devices, on_device(): panels = lax.all_gather(mine, 'col')  78.4 us
    all_to_all x1, blocking collectives, on_device(): lax.all_to_all(pieces, 'col', split_axis=0, concat_axis=0, tiled=True)  52.7 us
    psum x1, waiting for transfers between devices, on_device(): rhs = lax.psum(inner_dot(panels, stacked), 'row')  46.4 us
    dot_general x2, matrix products, inner_dot(): return lax.dot_general(left, right, (((0,), (0,)), ((), ())), precision=HI)  23.8 us
    another operation x14, matrix products, on_device(): lower = jnp.linalg.cholesky(gram, symmetrize_input=False)  23.3 us
  transfers between devices with their start and end apart: 3, of which 3 were waited for; matrix products, arithmetic and copies ran while one was open for 0% of the time, Pallas kernels for 0%

commit v1 on v0

--- a/solution.py
+++ b/solution.py
@@ -2,6 +2,7 @@
 import jax.numpy as jnp
 from jax import lax
 from jax.sharding import PartitionSpec as P
+from jax.lax import all_to_all, axis_size
 
 B = 256
 P_SIZE = 4
@@ -38,7 +39,9 @@
     share = lead // n_col
     own = lax.dynamic_slice(panels, (0, col_index * share), (height, share))
     gram_part = lax.psum(inner_dot(own, panels), "row")
-    gram = lax.all_gather(gram_part, "col", tiled=True)
+    gram = jnp.concatenate(
+        all_to_all(jnp.stack([gram_part] * axis_size("col"), axis=0), "col", 0, 0), 0
+    )
     rhs = lax.psum(inner_dot(panels, stacked), "row")
     lower = jnp.linalg.cholesky(gram, symmetrize_input=False)
     factor = jax.scipy.linalg.solve_triangular(lower, rhs, lower=True)

time: 647 us -> 675 us (1.043)
  starting transfers between devices: 0.09 us -> 12 us
  waiting for transfers between devices: 210 us -> 221 us
    all_to_all x0 -> x1, waiting for transfers between devices: none -> 95.8 us  [on_device(): all_to_all(jnp.stack([gram_part] * axis_size('col'), axis=0), 'col', 0, 0)]
    all_gather x1 -> x0, waiting for transfers between devices: 84.7 us -> none  [on_device(): gram = lax.all_gather(gram_part, 'col', tiled=True)]
    all_to_all x0 -> x1, starting transfers between devices: none -> 12 us  [on_device(): all_to_all(jnp.stack([gram_part] * axis_size('col'), axis=0), 'col', 0, 0)]
    another operation x24 -> x25, local copies, waits for them, and re-layouts: 22.8 us -> 26.2 us
where the time goes in v1:
time: 675 us; the launch traced here: 664 us
  other arithmetic  261 us (39%)
  waiting for transfers between devices  221 us (33%)
  matrix products  60 us (9%)
  blocking collectives  52.7 us (8%)
  local copies, waits for them, and re-layouts  38.1 us (6%)
  between operations  19.1 us (3%)
  starting transfers between devices  12 us (2%)
    another operation x30, other arithmetic, on_device(): lower = jnp.linalg.cholesky(gram, symmetrize_input=False)  173 us
    all_to_all x1, waiting for transfers between devices, on_device(): all_to_all(jnp.stack([gram_part] * axis_size('col'), axis=0), 'col', 0, 0)  95.8 us
    another operation x3, other arithmetic, on_device(): factor = jax.scipy.linalg.solve_triangular(lower, rhs, lower=True)  83.6 us
    all_gather x1, waiting for transfers between devices, on_device(): panels = lax.all_gather(mine, 'col')  78.4 us
    all_to_all x1, blocking collectives, on_device(): lax.all_to_all(pieces, 'col', split_axis=0, concat_axis=0, tiled=True)  52.7 us
    psum x1, waiting for transfers between devices, on_device(): rhs = lax.psum(inner_dot(panels, stacked), 'row')  46.4 us
    dot_general x2, matrix products, inner_dot(): return lax.dot_general(left, right, (((0,), (0,)), ((), ())), precision=HI)  24.6 us
    another operation x14, matrix products, on_device(): lower = jnp.linalg.cholesky(gram, symmetrize_input=False)  23.3 us
  transfers between devices with their start and end apart: 3, of which 3 were waited for; matrix products, arithmetic and copies ran while one was open for 0% of the time, Pallas kernels for 0%

profile of v1, /device:TPU:1, one launch (start us, length us, event | category | flops | bytes accessed | tf_op | source)
XLA Modules:
  0.0 664.0 jit_solution(102291230653934204)
XLA Ops:
  8.7 2.1 pad_maximum_fusion
  12.2 52.7 %all_to_all.10 = f32[64,20,256]{2,1,0:T(8,128)S(1)} all-to-all(f32[64,20,256]{2,1,0:T(8,128)S(1)} %reshape.95), channel_id=1, replica_groups=mesh['col'=64,'row'=4] {'col'}, dimensions={0} | all-to-all | bytes 2621440 | tf_op jit(solution)/shard_map/all_to_all | solution.py:35
  65.7 78.4 %all-gather.3.cloned.1.call-done = f32[256,20,256]{2,1,0:T(8,128)} async-done(((f32[4,20,256]{2,1,0:T(8,128)}), f32[256,20,256]{2,1,0:T(8,128)}) %all-gather.3.cloned.1.call-update) | async-done | bytes 5242896 | tf_op jit(solution)/shard_map/all_gather | solution.py:37
  144.1 5.2 copy.5
  150.5 9.5 %fusion.63 = f32[1024,256]{1,0:T(8,128)} fusion(f32[1280,1024]{1,0:T(8,128)S(1)} %bitcast.109, f32[1024,256]{1,0:T(8,128)S(1)} %broadcast_multiply_fusion, f32[256,256]{1,0:T(8,128)S(1)} %copy-done), kind=kOutput, calls=%fused_computation.162 | convolution fusion | flops 4026859520 | bytes 7602176 | tf_op jit(solution)/shard_map/dot_general | solution.py:14
  160.1 15.1 %fusion.5 = f32[16,1024]{1,0:T(8,128)} fusion(f32[1280,1024]{1,0:T(8,128)S(1)} %bitcast.110, s32[]{:T(128)S(6)} %select_n.14), kind=kOutput, calls=%fused_computation.31 | convolution fusion | flops 251658240 | bytes 5963780 | tf_op jit(solution)/shard_map/dot_general | solution.py:14
  175.2 46.4 %all-reduce.4.cloned.1.call-done = (f32[1024,256]{1,0:T(8,128)}, f32[16,1024]{1,0:T(8,128)}) async-done(((f32[1024,256]{1,0:T(8,128)}, f32[16,1024]{1,0:T(8,128)}), (f32[1024,256]{1,0:T(8,128)}, f32[16,1024]{1,0:T(8,128)})) %all-reduce.4.cloned.1.call-update) | async-done | bytes 1114128 | tf_op jit(solution)/shard_map/psum | solution.py:45
  221.6 3.3 stack.2
  224.9 12.0 %all-to-all-start.1 = ((f32[64,16,1024]{2,1,0:T(8,128)}), f32[64,16,1024]{2,1,0:T(8,128)}, u32[]{:S(2)}, u32[]{:S(2)}) async-start(f32[64,16,1024]{2,1,0:T(8,128)} %stack.2), calls=%async_computation.1 | async-start | bytes 8388608 | tf_op jit(solution)/shard_map/all_to_all | solution.py:43
  236.9 95.8 %all-to-all-done.1 = f32[64,16,1024]{2,1,0:T(8,128)} async-done(((f32[64,16,1024]{2,1,0:T(8,128)}), f32[64,16,1024]{2,1,0:T(8,128)}, u32[]{:S(2)}, u32[]{:S(2)}) %all-to-all-start.1) | async-done | bytes 4194336 | tf_op jit(solution)/shard_map/all_to_all | solution.py:43
  333.6 11.7 %cholesky.223 = f32[128,128]{1,0:T(8,128)S(1)} custom-call(f32[128,128]{1,0:T(8,128)S(1)} %cholesky.580), custom_call_target="Cholesky" | custom-call | tf_op jit(solution)/shard_map/jit(cholesky)/cholesky | solution.py:46
  345.4 9.8 %custom-call.63 = f32[1,128,128]{1,2,0:T(8,128)S(1)} custom-call(f32[1,128,128]{2,1,0:T(8,128)S(1)} %get-tuple-element.71), custom_call_target="InvertDiagBlocksLowerTriangular" | custom-call | tf_op jit(solution)/shard_map/jit(cholesky)/cholesky | solution.py:46
  355.2 2.5 cholesky.255
  357.7 2.4 constant_dynamic-update-slice_fusion.31
  360.1 1.5 convolution_subtract_fusion
  361.6 11.7 %cholesky.244 = f32[128,128]{1,0:T(8,128)S(1)} custom-call(f32[128,128]{1,0:T(8,128)S(1)} %cholesky.584), custom_call_target="Cholesky" | custom-call | tf_op jit(solution)/shard_map/jit(cholesky)/cholesky | solution.py:46
  374.0 10.2 %custom-call.64 = f32[1,128,128]{1,2,0:T(8,128)S(1)} custom-call(f32[1,128,128]{2,1,0:T(8,128)S(1)} %get-tuple-element.68), custom_call_target="InvertDiagBlocksLowerTriangular" | custom-call | tf_op jit(solution)/shard_map/jit(cholesky)/cholesky | solution.py:46
  385.4 2.1 convolution_subtract_fusion.1
  387.5 11.7 %cholesky.468 = f32[128,128]{1,0:T(8,128)S(1)} custom-call(f32[128,128]{1,0:T(8,128)S(1)} %cholesky.589), custom_call_target="Cholesky" | custom-call | tf_op jit(solution)/shard_map/jit(cholesky)/cholesky | solution.py:46
  400.6 9.8 %custom-call.65 = f32[1,128,128]{1,2,0:T(8,128)S(1)} custom-call(f32[1,128,128]{2,1,0:T(8,128)S(1)} %get-tuple-element.65), custom_call_target="InvertDiagBlocksLowerTriangular" | custom-call | tf_op jit(solution)/shard_map/jit(cholesky)/cholesky | solution.py:46
  411.6 2.3 convolution_subtract_fusion.2
  413.9 11.9 %cholesky.487 = f32[128,128]{1,0:T(8,128)S(1)} custom-call(f32[128,128]{1,0:T(8,128)S(1)} %cholesky.594), custom_call_target="Cholesky" | custom-call | tf_op jit(solution)/shard_map/jit(cholesky)/cholesky | solution.py:46
  427.1 9.8 %custom-call.66 = f32[1,128,128]{1,2,0:T(8,128)S(1)} custom-call(f32[1,128,128]{2,1,0:T(8,128)S(1)} %get-tuple-element.62), custom_call_target="InvertDiagBlocksLowerTriangular" | custom-call | tf_op jit(solution)/shard_map/jit(cholesky)/cholesky | solution.py:46
  438.1 2.3 convolution_subtract_fusion.3
  440.4 11.7 %cholesky.506 = f32[128,128]{1,0:T(8,128)S(1)} custom-call(f32[128,128]{1,0:T(8,128)S(1)} %cholesky.599), custom_call_target="Cholesky" | custom-call | tf_op jit(solution)/shard_map/jit(cholesky)/cholesky | solution.py:46
  453.5 9.8 %custom-call.67 = f32[1,128,128]{1,2,0:T(8,128)S(1)} custom-call(f32[1,128,128]{2,1,0:T(8,128)S(1)} %get-tuple-element.59), custom_call_target="InvertDiagBlocksLowerTriangular" | custom-call | tf_op jit(solution)/shard_map/jit(cholesky)/cholesky | solution.py:46
  464.3 2.5 convolution_subtract_fusion.4
  466.9 11.7 %cholesky.526 = f32[128,128]{1,0:T(8,128)S(1)} custom-call(f32[128,128]{1,0:T(8,128)S(1)} %cholesky.604), custom_call_target="Cholesky" | custom-call | tf_op jit(solution)/shard_map/jit(cholesky)/cholesky | solution.py:46
  479.9 9.8 %custom-call.68 = f32[1,128,128]{1,2,0:T(8,128)S(1)} custom-call(f32[1,128,128]{2,1,0:T(8,128)S(1)} %get-tuple-element.56), custom_call_target="InvertDiagBlocksLowerTriangular" | custom-call | tf_op jit(solution)/shard_map/jit(cholesky)/cholesky | solution.py:46
  490.6 2.0 convolution_subtract_fusion.11
  492.7 11.7 %cholesky.546 = f32[128,128]{1,0:T(8,128)S(1)} custom-call(f32[128,128]{1,0:T(8,128)S(1)} %cholesky.609), custom_call_target="Cholesky" | custom-call | tf_op jit(solution)/shard_map/jit(cholesky)/cholesky | solution.py:46
  505.7 10.2 %custom-call.69 = f32[1,128,128]{1,2,0:T(8,128)S(1)} custom-call(f32[1,128,128]{2,1,0:T(8,128)S(1)} %get-tuple-element.53), custom_call_target="InvertDiagBlocksLowerTriangular" | custom-call | tf_op jit(solution)/shard_map/jit(cholesky)/cholesky | solution.py:46
  516.7 1.8 convolution_subtract_fusion.13
  518.5 11.7 %cholesky.564 = f32[128,128]{1,0:T(8,128)S(1)} custom-call(f32[128,128]{1,0:T(8,128)S(1)} %convolution_subtract_fusion.13), custom_call_target="Cholesky" | custom-call | tf_op jit(solution)/shard_map/jit(cholesky)/cholesky | solution.py:46
  537.3 4.9 select_select_fusion
  542.2 23.0 %while.1 = (s32[]{:T(128)}, f32[1024,1024]{1,0:T(8,128)}, s32[8,2]{0,1:T(2,128)S(1)}, f32[8,128,128]{2,1,0:T(8,128)S(1)}, s32[]{:T(128)}) while((s32[]{:T(128)}, f32[1024,1024]{1,0:T(8,128)}, s32[8,2]{0,1:T(2,128)S(1)}, f32[8,128,128]{2,1,0:T(8,128)S(1)}, s32[]{:T(128)}) %tuple.58), condition=%wide.while_cond, body=%wide.while_body.sunk | while | flops 2 | bytes 131181 | solution.py:47
  542.8 2.3 bitcast_dynamic-update-slice_fusion.2
  545.7 2.3 bitcast_dynamic-update-slice_fusion.2
  548.6 2.3 bitcast_dynamic-update-slice_fusion.2
  551.5 2.3 bitcast_dynamic-update-slice_fusion.2
  554.3 2.3 bitcast_dynamic-update-slice_fusion.2
  557.2 2.3 bitcast_dynamic-update-slice_fusion.2
  560.1 2.3 bitcast_dynamic-update-slice_fusion.2
  563.0 2.2 bitcast_dynamic-update-slice_fusion.2
  565.2 78.8 %custom-call.70 = f32[8,128,128]{1,2,0:T(8,128)S(1)} custom-call(f32[8,128,128]{2,1,0:T(8,128)S(1)} %get-tuple-element.12), custom_call_target="InvertDiagBlocksLowerTriangular" | custom-call | tf_op jit(solution)/shard_map/jit(_solve_triangular)/triangular_solve | solution.py:47
  650.6 1.5 convolution_subtract_fusion.5
  652.4 1.5 convolution_subtract_fusion.9
  654.2 1.6 convolution_subtract_fusion.12
  (75 shorter events, 35.2 us)
Async XLA Ops:
  6.5 137.5 %all-gather.3.cloned.1.call-start = ((), (), s32[]{:S(2)}) async-start(), calls=%async_computation.2 | async-start | bytes 6389760 | tf_op jit(solution)/shard_map/all_gather | solution.py:37
  65.6 156.0 %all-reduce.4.cloned.1.call-start = ((), (), s32[]{:S(2)}) async-start(), calls=%async_computation.3 | async-start | bytes 2228224 | tf_op jit(solution)/shard_map/psum | solution.py:45
  149.2 1.3 copy-start
  224.9 107.9 %all-to-all-start.1 = ((f32[64,16,1024]{2,1,0:T(8,128)}), f32[64,16,1024]{2,1,0:T(8,128)}, u32[]{:S(2)}, u32[]{:S(2)}) async-start(f32[64,16,1024]{2,1,0:T(8,128)} %stack.2), calls=%async_computation.1 | async-start | bytes 8388608 | tf_op jit(solution)/shard_map/all_to_all | solution.py:43
  537.3 106.7 %copy-start.1 = (f32[1024,256]{1,0:T(8,128)S(1)}, f32[1024,256]{1,0:T(8,128)}, u32[]{:S(2)}) copy-start(f32[1024,256]{1,0:T(8,128)} %get-tuple-element.21) | copy-start | bytes 3145732
Sparse Core Ops, SparseCore 0:
  65.7 78.2 all-gather.2
  175.3 46.2 all-reduce.3
